TPU v7x, 512 devices: a whole 4x8x8 slice. The times are simulated.
512 devices in a mesh: dom: 16 (over x, z_hi, core), ctx: 32 (over z_lo, y).
Axes of the slice: x: 4, y: 8, z: 8 (z_hi: 2, z_lo: 4; z = z_hi * 4 + z_lo), core: 2. Of those that a mesh axis runs over, the one named last changes fastest.
Arguments:
- q_new: bfloat16 [65536, 4096], P(('dom', 'ctx')), may hold values from -40 to 40
- kv_new: bfloat16 [65536, 2, 512], P(('dom', 'ctx')), may hold values from -5 to 5
- prompt_kv: bfloat16 [2048, 2, 512], P('ctx'), may hold values from -5 to 5
- cache_kv: bfloat16 [512, 256, 2, 512], P('dom', 'ctx'), may hold values from -5 to 5
- ancestors: int32 [512], replicated, may hold values from 0 to 511, as said below
- lengths: int32 [512], replicated, may hold values from 1 to 32, as said below
Outputs:
- attended: bfloat16 [65536, 4096], P(('dom', 'ctx'))
Inputs may be any that keep to these rules, and one draw needn't show every extreme that they name: The 512 particles form 16 groups of 32 consecutive ones; within a group, each run of 4 consecutive particles takes all its ancestors from one group, and the runs of a group take them from different groups (its own among the possible ones). Ancestors repeat freely. `lengths`: both ends are reached.
All inputs are finite; a program needn't handle non-finite values.
Results may differ from a plain program's by a relative error of at most 0.022.
Values may be sent and summed in bfloat16 or wider, within the bound.
A program may use at most 128 MiB of HBM per device.

v0:
```python
import jax
import jax.numpy as jnp
from jax import lax
from jax.sharding import PartitionSpec as P

HD = 128
H = 32
KVH = 4
SPAN = 128
PAGE = 8
GQ = 8


NEGATIVE = -1e30


def fresh_state(leading):
    return (
        jnp.full(leading, NEGATIVE, jnp.float32),
        jnp.zeros(leading, jnp.float32),
        jnp.zeros(leading + (HD,), jnp.float32),
    )


def absorb(running, queries, key_part, value_part, visible):
    maxima, totals, accumulated = running
    scores = jnp.einsum(
        "rgjd,kgd->rgjk", queries, key_part, preferred_element_type=jnp.float32
    ) * HD ** (-0.5)
    if visible is not None:
        scores = jnp.where(visible, scores, NEGATIVE)
    new_max = jnp.maximum(maxima, jnp.max(scores, axis=-1))
    weights = jnp.exp(scores - new_max[..., None])
    if visible is not None:
        weights = jnp.where(visible, weights, 0.0)
    factor = jnp.exp(maxima - new_max)
    totals = factor * totals + jnp.sum(weights, axis=-1)
    accumulated = factor[..., None] * accumulated + jnp.einsum(
        "rgjk,kgd->rgjd",
        weights.astype(jnp.bfloat16),
        value_part,
        preferred_element_type=jnp.float32,
    )
    return (new_max, totals, accumulated)


def absorb_blocks(running, queries, key_rows, value_rows, visible):
    query_count = queries.shape[0] * queries.shape[1] * queries.shape[2]
    key_block = max(128, 2**21 // query_count)
    length = key_rows.shape[0]
    for begin_at in range(0, length, key_block):
        end_at = min(begin_at + key_block, length)
        window = None if visible is None else visible
        running = absorb(
            running, queries, key_rows[begin_at:end_at], value_rows[begin_at:end_at], window
        )
    return running


def on_device(q_new, kv_new, prompt_kv, cache_kv, ancestors, lengths):
    dom_count = lax.axis_size("dom")
    ctx_count = lax.axis_size("ctx")
    dom_index = lax.axis_index("dom")
    ctx_index = lax.axis_index("ctx")
    group_size = cache_kv.shape[0]
    per_device = group_size // ctx_count
    capacity = 2 * group_size // dom_count
    page_rows = cache_kv.shape[1]
    kv_width = cache_kv.shape[3]
    source_group = (ancestors // group_size).reshape(dom_count, group_size)
    source_local = (ancestors % group_size).reshape(dom_count, group_size)
    from_here = (source_group == dom_index).astype(jnp.int32)
    ranking = jnp.cumsum(from_here, axis=1) - 1
    slot_ids = jnp.arange(capacity, dtype=jnp.int32)
    chosen = (from_here[:, :, None] == 1) & (ranking[:, :, None] == slot_ids[None, None, :])
    slot_local = jnp.sum(jnp.where(chosen, source_local[:, :, None], 0), axis=1)
    outgoing = cache_kv[slot_local.reshape(-1)].reshape(dom_count, capacity, page_rows, 2, kv_width)
    incoming = lax.all_to_all(outgoing, "dom", split_axis=0, concat_axis=0, tiled=True)
    own_source = lax.dynamic_index_in_dim(source_group, dom_index, 0, keepdims=False)
    group_ids = jnp.arange(dom_count, dtype=jnp.int32)
    matches = (own_source[:, None] == group_ids[None, :]).astype(jnp.int32)
    own_rank = jnp.sum(matches * (jnp.cumsum(matches, axis=0) - 1), axis=1)
    copied = incoming.reshape(dom_count * capacity, page_rows, 2, kv_width)[
        own_source * capacity + own_rank
    ]
    gathered_pages = lax.all_to_all(copied, "ctx", split_axis=0, concat_axis=1, tiled=True)
    particle_ids = (
        dom_index * group_size + ctx_index * per_device + jnp.arange(per_device, dtype=jnp.int32)
    )
    anchors = jnp.take(ancestors, particle_ids)
    page_limit = jnp.take(lengths, anchors) * PAGE
    row_count = per_device * SPAN
    queries = q_new.reshape(row_count, KVH, GQ, HD)
    fresh_kv = kv_new.reshape(per_device, SPAN, 2, KVH, HD)
    positions = jnp.arange(SPAN, dtype=jnp.int32)
    causal = (positions[None, :] <= positions[:, None])[:, None, None, :]
    gen_rows = gathered_pages.shape[1]
    cache_positions = jnp.arange(gen_rows, dtype=jnp.int32)
    running = fresh_state((SPAN, KVH, GQ))
    running = absorb_blocks(running, queries, fresh_kv[0, :, 0], fresh_kv[0, :, 1], causal)
    member_pages = gathered_pages[0].reshape(gen_rows, 2, KVH, HD)
    visible = (cache_positions < page_limit[0])[None, None, None, :]
    running = absorb_blocks(running, queries, member_pages[:, 0], member_pages[:, 1], visible)
    pieces = [running]
    local_state = tuple(
        (
            jnp.concatenate([member_state[number] for member_state in pieces], axis=0)
            for number in range(3)
        )
    )
    shard_rows = lax.all_gather(prompt_kv, "ctx", axis=0, tiled=True)
    shard_kv = shard_rows.reshape(shard_rows.shape[0], 2, KVH, HD)
    final_state = absorb_blocks(local_state, queries, shard_kv[:, 0], shard_kv[:, 1], None)
    output = (final_state[2] / final_state[1][..., None]).astype(jnp.bfloat16)
    return output.reshape(row_count, H * HD)


def solution(mesh):
    placed = (
        P(("dom", "ctx"), None),
        P(("dom", "ctx"), None, None),
        P("ctx", None, None),
        P("dom", "ctx", None, None),
        P(),
        P(),
    )
    return jax.shard_map(
        on_device, mesh=mesh, in_specs=placed, out_specs=P(("dom", "ctx"), None), check_vma=False
    )
```

profile of v0, /device:TPU:6, one launch (start us, length us, event | category | flops | bytes accessed | tf_op | source)
XLA Modules:
  0.0 229.8 jit_solution(18023625704253023764)
XLA Ops:
  6.5 0.7 all-gather.2.cloned.1.call-update
  7.3 0.7 add_select_fusion.1
  8.7 2.7 %gather_fusion = bf16[64,8,2,512]{3,2,1,0:T(2,128)(2,1)S(1)} fusion(bf16[32,8,2,512]{3,2,1,0:T(2,128)(2,1)S(1)} %copy-done, s32[1024]{0:T(1024)S(1)} %pad_clamp_fusion.1), kind=kCustom, calls=%fused_computation | custom fusion | bytes 2097408 | tf_op jit(solution)/shard_map/gather | solution.py:77
  11.4 1.2 copy.100
  12.6 13.2 %all-to-all-start = ((bf16[16,4,8,2,512]{4,2,3,1,0:T(8,128)(2,1)}), bf16[16,4,8,2,512]{4,2,3,1,0:T(8,128)(2,1)S(1)}, u32[]{:S(2)}, u32[]{:S(2)}) async-start(bf16[16,4,8,2,512]{4,2,3,1,0:T(8,128)(2,1)} %copy.100), calls=%async_computation | async-start | bytes 2097152 | tf_op jit(solution)/shard_map/all_to_all | solution.py:78
  26.2 25.2 %all-to-all-done = bf16[16,4,8,2,512]{4,2,3,1,0:T(8,128)(2,1)S(1)} async-done(((bf16[16,4,8,2,512]{4,2,3,1,0:T(8,128)(2,1)}), bf16[16,4,8,2,512]{4,2,3,1,0:T(8,128)(2,1)S(1)}, u32[]{:S(2)}, u32[]{:S(2)}) %all-to-all-start) | async-done | bytes 1048608 | tf_op jit(solution)/shard_map/all_to_all | solution.py:78
  51.4 1.4 gather_fusion.1
  52.8 24.5 %all-to-all-start.1 = ((bf16[32,8,2,512]{3,1,2,0:T(8,128)(2,1)}), bf16[32,8,2,512]{3,1,2,0:T(8,128)(2,1)S(1)}, u32[]{:S(2)}, u32[]{:S(2)}) async-start(bf16[32,8,2,512]{3,1,2,0:T(8,128)(2,1)} %gather_fusion.1), calls=%async_computation.1 | async-start | bytes 1048576 | tf_op jit(solution)/shard_map/all_to_all | solution.py:86
  77.3 1.3 dynamic-slice.4
  79.4 1.5 copy.146
  80.9 1.3 dynamic-slice.5
  82.9 2.0 fusion.47
  84.9 12.8 %all-to-all-done.1 = bf16[32,8,2,512]{3,1,2,0:T(8,128)(2,1)S(1)} async-done(((bf16[32,8,2,512]{3,1,2,0:T(8,128)(2,1)}), bf16[32,8,2,512]{3,1,2,0:T(8,128)(2,1)S(1)}, u32[]{:S(2)}, u32[]{:S(2)}) %all-to-all-start.1) | async-done | bytes 524320 | tf_op jit(solution)/shard_map/all_to_all | solution.py:86
  98.2 3.0 %bitcast_reduce_fusion.4 = (f32[128,4,8]{0,2,1:T(8,128)S(1)}, f32[4,256,128,8]{2,1,3,0:T(8,128)}) fusion(pred[256]{0:T(512)(128)(4,1)S(1)} %iota_compare_fusion.3, bf16[128,4,8,128]{3,2,1,0:T(8,128)(2,1)S(1)} %bitcast.219, bf16[256,1,4,128]{3,2,0,1:T(4,128)(2,1)S(1)} %get-tuple-element.41), kind=kOutput, calls=%fused_computation.27 | convolution fusion | flops 271577088 | bytes 5521664 | tf_op jit(solution)/shard_map/rgjd,kgd->rgjk/dot_general | solution.py:27
  101.2 79.5 %all-gather.2.cloned.1.call-done = bf16[2048,2,512]{2,1,0:T(2,128)(2,1)} async-done(((bf16[64,2,512]{2,1,0:T(2,128)(2,1)}), bf16[2048,2,512]{2,1,0:T(2,128)(2,1)}) %all-gather.2.cloned.1.call-update) | async-done | bytes 4194320 | tf_op jit(solution)/shard_map/all_gather | solution.py:111
  180.7 11.2 %copy.104 = bf16[2048,2,512]{0,2,1:T(8,128)(2,1)} copy(bf16[2048,2,512]{2,1,0:T(2,128)(2,1)} %all-gather.2.cloned.1.call-done) | data formatting | bytes 8388608 | tf_op jit(solution)/shard_map/all_gather | solution.py:111
  191.9 2.6 %bitcast_reduce_fusion.3 = (f32[128,4,8]{0,2,1:T(8,128)S(1)}, f32[4,512,128,8]{2,1,3,0:T(8,128)S(1)}) fusion(bf16[128,4,8,128]{3,2,1,0:T(8,128)(2,1)S(1)} %bitcast.220, bf16[2048,2,4,128]{0,3,2,1:T(8,128)(2,1)} %bitcast.224), kind=kOutput, calls=%fused_computation.12 | convolution fusion | flops 541061120 | bytes 9977856 | tf_op jit(solution)/shard_map/rgjd,kgd->rgjk/dot_general | solution.py:27
  194.5 1.4 bitcast_reduce_fusion.2
  195.9 1.4 bitcast_reduce_fusion.1
  197.3 1.4 bitcast_reduce_fusion
  198.7 3.0 %fusion.12 = f32[4,128,8,128]{1,3,2,0:T(8,128)} fusion(f32[4,512,128,8]{2,1,3,0:T(8,128)S(1)} %get-tuple-element.47, f32[128,4,8]{0,2,1:T(8,128)S(1)} %get-tuple-element.33, bf16[2048,2,4,128]{0,3,2,1:T(8,128)(2,1)S(1)} %bitcast.231), kind=kOutput, calls=%fused_computation.22 | convolution fusion | flops 543162368 | bytes 11026432 | tf_op jit(solution)/shard_map/rgjk,kgd->rgjd/dot_general | solution.py:38
  201.7 3.3 %fusion.8 = (f32[128,4,8]{0,2,1:T(8,128)S(1)}, f32[128,4,8]{0,2,1:T(8,128)S(1)}) fusion(f32[4,512,128,8]{2,1,3,0:T(8,128)S(1)} %get-tuple-element.49, f32[128,4,8]{0,2,1:T(8,128)S(1)} %get-tuple-element.34, f32[128,4,8]{0,2,1:T(8,128)S(1)} %get-tuple-element.33, f32[4,512,128,8]{2,1,3,0:T(8,128)S(1)} %get-tuple-element.47), kind=kLoop, calls=%fused_computation.18 | loop fusion | flops 12574720 | bytes 16842752 | tf_op jit(solution)/shard_map/reduce_sum | solution.py:37
  205.1 2.7 %fusion.14 = f32[4,128,8,128]{1,3,2,0:T(8,128)S(1)} fusion(f32[4,512,128,8]{2,1,3,0:T(8,128)S(1)} %get-tuple-element.49, f32[128,4,8]{0,2,1:T(8,128)S(1)} %get-tuple-element.34, bf16[2048,2,4,128]{0,3,2,1:T(8,128)(2,1)} %bitcast.225), kind=kOutput, calls=%fused_computation.23 | convolution fusion | flops 543162368 | bytes 11026432 | tf_op jit(solution)/shard_map/rgjk,kgd->rgjd/dot_general | solution.py:38
  207.8 2.7 %fusion.16 = f32[4,128,8,128]{1,3,2,0:T(8,128)S(1)} fusion(f32[4,512,128,8]{2,1,3,0:T(8,128)S(1)} %get-tuple-element.51, f32[128,4,8]{0,2,1:T(8,128)S(1)} %get-tuple-element.35, bf16[2048,2,4,128]{0,3,2,1:T(8,128)(2,1)} %bitcast.226), kind=kOutput, calls=%fused_computation.24 | convolution fusion | flops 543162368 | bytes 11026432 | tf_op jit(solution)/shard_map/rgjk,kgd->rgjd/dot_general | solution.py:38
  210.5 3.1 %fusion.4 = (f32[128,4,8]{0,2,1:T(8,128)S(1)}, f32[128,4,8]{0,2,1:T(8,128)S(1)}) fusion(f32[4,512,128,8]{2,1,3,0:T(8,128)S(1)} %get-tuple-element.53, f32[128,4,8]{0,2,1:T(8,128)S(1)} %get-tuple-element.36, f32[128,4,8]{0,2,1:T(8,128)S(1)} %get-tuple-element.35, f32[4,512,128,8]{2,1,3,0:T(8,128)S(1)} %get-tuple-element.51), kind=kLoop, calls=%fused_computation.14 | loop fusion | flops 12574720 | bytes 16842752 | tf_op jit(solution)/shard_map/reduce_sum | solution.py:37
  213.7 2.9 %fusion.18 = f32[4,128,8,128]{1,3,2,0:T(8,128)S(1)} fusion(f32[4,512,128,8]{2,1,3,0:T(8,128)S(1)} %get-tuple-element.53, f32[128,4,8]{0,2,1:T(8,128)S(1)} %get-tuple-element.36, bf16[2048,2,4,128]{0,3,2,1:T(8,128)(2,1)} %bitcast.227), kind=kOutput, calls=%fused_computation.25 | convolution fusion | flops 543162368 | bytes 11026432 | tf_op jit(solution)/shard_map/rgjk,kgd->rgjd/dot_general | solution.py:38
  216.6 1.2 fusion.30
  217.8 1.2 fusion.32
  219.0 0.4 copy-done.4
  219.4 0.6 fusion.48
  220.0 1.7 fusion.35
  221.7 1.3 copy.120
  (39 shorter events, 1.9 us)
Async XLA Ops:
  6.5 2.1 copy-start
  6.5 174.2 %all-gather.2.cloned.1.call-start = ((), (), s32[]{:S(2)}) async-start(), calls=%async_computation.2 | async-start | bytes 4325376 | tf_op jit(solution)/shard_map/all_gather | solution.py:111
  8.7 70.5 %copy-start.6 = (bf16[128,2,512]{2,1,0:T(2,128)(2,1)S(1)}, bf16[128,2,512]{2,1,0:T(2,128)(2,1)}, u32[]{:S(2)}) copy-start(bf16[128,2,512]{2,1,0:T(2,128)(2,1)} %param.7) | copy-start | bytes 786436
  12.6 38.8 %all-to-all-start = ((bf16[16,4,8,2,512]{4,2,3,1,0:T(8,128)(2,1)}), bf16[16,4,8,2,512]{4,2,3,1,0:T(8,128)(2,1)S(1)}, u32[]{:S(2)}, u32[]{:S(2)}) async-start(bf16[16,4,8,2,512]{4,2,3,1,0:T(8,128)(2,1)} %copy.100), calls=%async_computation | async-start | bytes 2097152 | tf_op jit(solution)/shard_map/all_to_all | solution.py:78
  52.8 44.9 %all-to-all-start.1 = ((bf16[32,8,2,512]{3,1,2,0:T(8,128)(2,1)}), bf16[32,8,2,512]{3,1,2,0:T(8,128)(2,1)S(1)}, u32[]{:S(2)}, u32[]{:S(2)}) async-start(bf16[32,8,2,512]{3,1,2,0:T(8,128)(2,1)} %gather_fusion.1), calls=%async_computation.1 | async-start | bytes 1048576 | tf_op jit(solution)/shard_map/all_to_all | solution.py:86
  191.9 2.6 %copy-start.3 = (bf16[2048,2,512]{0,2,1:T(8,128)(2,1)S(1)}, bf16[2048,2,512]{0,2,1:T(8,128)(2,1)}, u32[]{:S(2)}) copy-start(bf16[2048,2,512]{0,2,1:T(8,128)(2,1)} %copy.104) | copy-start | bytes 12582916
  213.7 2.9 %copy-start.2 = (f32[4,256,128,8]{2,1,3,0:T(8,128)S(1)}, f32[4,256,128,8]{2,1,3,0:T(8,128)}, u32[]{:S(2)}) copy-start(f32[4,256,128,8]{2,1,3,0:T(8,128)} %get-tuple-element.55) | copy-start | bytes 12582916
  217.8 1.6 copy-start.4
  217.8 2.2 copy-start.5
  220.0 3.0 %copy-start.1 = (bf16[32,8,2,512]{3,2,1,0:T(2,128)(2,1)S(1)}, bf16[32,8,2,512]{3,2,1,0:T(2,128)(2,1)}, u32[]{:S(2)}) copy-start(bf16[32,8,2,512]{3,2,1,0:T(2,128)(2,1)} %param.9) | copy-start | bytes 1572868
Sparse Core Ops, SparseCore 0:
  9.4 171.2 all-gather.1
where the time goes:
time: 231 us; the launch traced here: 230 us
  waiting for transfers between devices  118 us (51%)
  starting transfers between devices  37.7 us (16%)
  matrix products  25.9 us (11%)
  local copies, waits for them, and re-layouts  23.4 us (10%)
  between operations  14.9 us (6%)
  other arithmetic  9.66 us (4%)
    all_gather x1, waiting for transfers between devices, on_device(): shard_rows = lax.all_gather(prompt_kv, 'ctx', axis=0, tiled=True)  79.5 us
    all_to_all x1, waiting for transfers between devices, on_device(): lax.all_to_all(outgoing, 'dom', split_axis=0, concat_axis=0, tiled=True)  25.2 us
    all_to_all x1, starting transfers between devices, on_device(): lax.all_to_all(copied, 'ctx', split_axis=0, concat_axis=1, tiled=True)  24.5 us
    dot_general x6, matrix products, absorb(): jnp.einsum('rgjk,kgd->rgjd', weights.astype(jnp.bfloat16), value_part, pr...  14.2 us
    all_to_all x1, starting transfers between devices, on_device(): lax.all_to_all(outgoing, 'dom', split_axis=0, concat_axis=0, tiled=True)  13.2 us
    all_to_all x1, waiting for transfers between devices, on_device(): lax.all_to_all(copied, 'ctx', split_axis=0, concat_axis=1, tiled=True)  12.8 us
    dot_general x6, matrix products, absorb(): jnp.einsum('rgjd,kgd->rgjk', queries, key_part, preferred_element_type=jn...  11.7 us
    all_gather x1, local copies, waits for them, and re-layouts, on_device(): shard_rows = lax.all_gather(prompt_kv, 'ctx', axis=0, tiled=True)  11.2 us
  transfers between devices with their start and end apart: 3, of which 3 were waited for; matrix products, arithmetic and copies ran while one was open for 7% of the time, Pallas kernels for 0%

commit v1 on v0

v1 whole, which is shorter than its diff:
```python
import functools

import jax
import jax.numpy as jnp
from jax import lax
from jax.experimental import pallas as pl
from jax.experimental.pallas import tpu as pltpu
from jax.sharding import PartitionSpec as P

HD = 128
H = 32
KVH = 4
SPAN = 128
PAGE = 8
GQ = 8
NDOM = 16
NCTX = 32
NY = 8
NZLO = 4
PG = 32
CAP = 4
SHARD = 64
ZBLOCK = SHARD * NZLO
KVW = KVH * HD
ROWS = 2 * PAGE
NEGATIVE = -1e30
SCALE = HD ** (-0.5) * 1.4426950408889634


def place():
    dom = lax.axis_index("dom")
    ctx = lax.axis_index("ctx")
    core = dom % 2
    z_hi = (dom // 2) % 2
    x = dom // 4
    z_lo = ctx // NY
    y = ctx % NY
    return dom, ctx, x, z_hi, core, z_lo, y


def at_z(x, core, y, z):
    z = z % (2 * NZLO)
    return {"dom": (x * 2 + z // NZLO) * 2 + core, "ctx": (z % NZLO) * NY + y}


def rcopy(src, dst, send, recv, target):
    return pltpu.make_async_remote_copy(
        src_ref=src,
        dst_ref=dst,
        send_sem=send,
        recv_sem=recv,
        device_id=target,
        device_id_type=pl.DeviceIdType.MESH,
    )


def exchange_kernel(
    anc, prompt, cache, pk, gbuf, sbuf, rbuf, tbuf,
    z_send, z_recv, r_send, r_recv, l_send, l_recv, c_send, c_recv, d_send, d_recv, p_send, p_recv,
):
    dom, ctx, x, z_hi, core, z_lo, y = place()
    z = z_hi * NZLO + z_lo
    sibling = {"dom": dom + 1 - 2 * core, "ctx": ctx}
    right = {"dom": dom, "ctx": z_lo * NY + (y + 1) % NY}
    left = {"dom": dom, "ctx": z_lo * NY + (y + NY - 1) % NY}
    far = 2 - 4 * (z % 2)
    z_targets = [at_z(x, core, y, z + 1), at_z(x, core, y, z + 7), at_z(x, core, y, z + far + 8)]

    barrier = pltpu.get_barrier_semaphore()

    def greet(target):
        pl.semaphore_signal(barrier, inc=1, device_id=target, device_id_type=pl.DeviceIdType.MESH)

    for target in (z_targets[0], z_targets[1], at_z(x, core, y, z - far + 8)):
        greet(target)

    def greet_dom(o, carry):
        greet({"dom": (dom + o) % NDOM, "ctx": ctx})
        return carry

    def greet_ctx(o, carry):
        greet({"dom": dom, "ctx": (ctx + o) % NCTX})
        return carry

    lax.fori_loop(1, NDOM, greet_dom, 0)
    lax.fori_loop(1, NCTX, greet_ctx, 0)
    pk[core, y, pl.ds(z_lo * SHARD, SHARD), :] = prompt[core]

    def pick(d, carry):
        run = 0
        for r in range(PG // CAP):
            run = jnp.where(anc[d * PG + r * CAP] // PG == dom, r, run)
        for k in range(CAP):
            local = anc[d * PG + run * CAP + k] % PG
            sbuf[d, pl.ds(k * ROWS, ROWS), :] = cache[local]
        return carry

    lax.fori_loop(0, NDOM, pick, 0)
    pl.semaphore_wait(barrier, 3 + NDOM - 1 + NCTX - 1)

    own_rows = pl.ds(z_lo * SHARD, SHARD)
    z_copies = [
        rcopy(pk.at[core, y, own_rows], pk.at[core, y, own_rows], z_send.at[i], z_recv.at[i], z_targets[i])
        for i in range(3)
    ]
    for copy in z_copies:
        copy.start()

    def dom_copy(o):
        d = (dom + o) % NDOM
        return rcopy(sbuf.at[d], rbuf.at[dom], d_send.at[o], d_recv.at[o], {"dom": d, "ctx": ctx})

    def start_dom(o, carry):
        dom_copy(o).start()
        return carry

    def wait_dom(o, carry):
        dom_copy(o).wait()
        return carry

    lax.fori_loop(1, NDOM, start_dom, 0)
    rbuf[dom] = sbuf[dom]

    def core_copy(i, yy):
        return rcopy(pk.at[core, yy], pk.at[core, yy], c_send.at[i], c_recv.at[i], sibling)

    for copy in z_copies:
        copy.wait()
    core_copies = [core_copy(0, y)]
    core_copies[0].start()
    half = ZBLOCK // 2
    rights, lefts = [], []
    for t in range(4):
        yr = (y + NY - t) % NY
        yl = (y + t) % NY
        if t > 0:
            rights[t - 1].wait_recv()
            lefts[t - 1].wait_recv()
        rrows = pl.ds(0, ZBLOCK if t < 3 else half)
        lrows = pl.ds(0 if t < 3 else half, ZBLOCK if t < 3 else half)
        rights.append(
            rcopy(pk.at[core, yr, rrows], pk.at[core, yr, rrows], r_send.at[t], r_recv.at[t], right)
        )
        lefts.append(
            rcopy(pk.at[core, yl, lrows], pk.at[core, yl, lrows], l_send.at[t], l_recv.at[t], left)
        )
        rights[t].start()
        lefts[t].start()
        if t > 0:
            for i, yy in ((2 * t - 1, yr), (2 * t, yl)):
                core_copies.append(core_copy(i, yy))
                core_copies[-1].start()
    rights[3].wait_recv()
    lefts[3].wait_recv()
    core_copies.append(core_copy(7, (y + 4) % NY))
    core_copies[-1].start()

    lax.fori_loop(1, NDOM, wait_dom, 0)

    def deal(i, carry):
        source = anc[dom * PG + i] // PG
        picked = rbuf[source, pl.ds(pl.multiple_of((i % CAP) * ROWS, ROWS), ROWS), :]
        tbuf[i] = picked
        return carry

    lax.fori_loop(0, PG, deal, 0)

    def ctx_copy(o):
        i = (ctx + o) % NCTX
        return rcopy(tbuf.at[i], gbuf.at[ctx], p_send.at[o], p_recv.at[o], {"dom": dom, "ctx": i})

    def start_ctx(o, carry):
        ctx_copy(o).start()
        return carry

    def wait_ctx(o, carry):
        ctx_copy(o).wait()
        return carry

    lax.fori_loop(1, NCTX, start_ctx, 0)
    gbuf[ctx] = tbuf[ctx]
    for t in range(4):
        rights[t].wait_send()
        lefts[t].wait_send()
    for copy in core_copies:
        copy.wait()
    lax.fori_loop(1, NCTX, wait_ctx, 0)


def exchange(anc, prompt, cache):
    vmem = pl.BlockSpec(memory_space=pltpu.VMEM)
    dma = pltpu.SemaphoreType.DMA
    return pl.pallas_call(
        exchange_kernel,
        out_shape=(
            jax.ShapeDtypeStruct((2, NY, ZBLOCK, KVW), jnp.bfloat16),
            jax.ShapeDtypeStruct((NCTX, ROWS, KVW), jnp.bfloat16),
        ),
        in_specs=[pl.BlockSpec(memory_space=pltpu.SMEM), vmem, vmem],
        out_specs=(vmem, vmem),
        scratch_shapes=[
            pltpu.VMEM((NDOM, CAP * ROWS, KVW), jnp.bfloat16),
            pltpu.VMEM((NDOM, CAP * ROWS, KVW), jnp.bfloat16),
            pltpu.VMEM((NCTX, ROWS, KVW), jnp.bfloat16),
            dma((3,)), dma((3,)), dma((4,)), dma((4,)), dma((4,)), dma((4,)),
            dma((8,)), dma((8,)), dma((NDOM,)), dma((NDOM,)), dma((NCTX,)), dma((NCTX,)),
        ],
        compiler_params=pltpu.CompilerParams(
            collective_id=0, has_side_effects=True, vmem_limit_bytes=40 * 2**20
        ),
        name="exchange",
    )(anc, prompt, cache)


BLOCK = 4 * SPAN


def queries_of(q, g, part):
    begin = g * GQ * HD + part * 4 * HD
    return jnp.concatenate(
        [q[:, pl.ds(pl.multiple_of(begin + j * HD, HD), HD)] for j in range(4)], axis=0
    )


def absorb(q, state, g, part, keys, values, visible, first):
    m_ref, l_ref, acc_ref = state
    n = keys.shape[0]
    scores = lax.dot_general(
        queries_of(q, g, part), keys, (((1,), (1,)), ((), ())), preferred_element_type=jnp.float32
    )
    if visible is not None:
        scores = jnp.where(visible, scores, NEGATIVE)
    top = jnp.max(scores, axis=1, keepdims=True)
    at = g * 2 + part
    if first:
        m_new = jnp.broadcast_to(top, (BLOCK, HD))
    else:
        m_old = m_ref[at]
        m_new = jnp.maximum(m_old, top)
    weights = jnp.concatenate(
        [jnp.exp2((scores[:, i * HD : (i + 1) * HD] - m_new) * SCALE) for i in range(n // HD)], axis=1
    )
    total = weights[:, :HD]
    for i in range(1, n // HD):
        total = total + weights[:, i * HD : (i + 1) * HD]
    added = jnp.dot(weights.astype(jnp.bfloat16), values, preferred_element_type=jnp.float32)
    if first:
        l_ref[at] = total
        acc_ref[at] = added
    else:
        factor = jnp.exp2((m_old - m_new) * SCALE)
        l_ref[at] = factor * l_ref[at] + total
        acc_ref[at] = factor * acc_ref[at] + added
    m_ref[at] = m_new


def absorb_new(q, kvn, state):
    def step(i, carry):
        g, part = i // 2, i % 2
        cols = pl.ds(pl.multiple_of(g * HD, HD), HD)
        row = lax.broadcasted_iota(jnp.int32, (BLOCK, SPAN), 0) % SPAN
        col = lax.broadcasted_iota(jnp.int32, (BLOCK, SPAN), 1)
        absorb(q, state, g, part, kvn[0, :, cols], kvn[1, :, cols], col <= row, True)
        return carry

    lax.fori_loop(0, 2 * KVH, step, 0)


def absorb_prompt(q, pk, state, blocks):
    def step(i, carry):
        g, part = i // 2, i % 2
        cols = pl.ds(pl.multiple_of(g * HD, HD), HD)
        keys = jnp.concatenate([pk[0, b, :, cols] for b in blocks], axis=0)
        values = jnp.concatenate([pk[1, b, :, cols] for b in blocks], axis=0)
        absorb(q, state, g, part, keys, values, None, False)
        return carry

    lax.fori_loop(0, 2 * KVH, step, 0)


def absorb_pages(q, gbuf, limit, state):
    def step(i, carry):
        g, part = i // 2, i % 2
        cols = pl.ds(pl.multiple_of(g * HD, HD), HD)
        pages = gbuf[:, :, cols].astype(jnp.float32)
        keys = pages[:, :PAGE].reshape(NCTX * PAGE, HD).astype(jnp.bfloat16)
        values = pages[:, PAGE:].reshape(NCTX * PAGE, HD).astype(jnp.bfloat16)
        col = lax.broadcasted_iota(jnp.int32, (BLOCK, NCTX * PAGE), 1)
        absorb(q, state, g, part, keys, values, col < limit, False)
        return carry

    lax.fori_loop(0, 2 * KVH, step, 0)


def finish(state, out):
    m_ref, l_ref, acc_ref = state

    def step(i, carry):
        result = acc_ref[i] / jnp.sum(l_ref[i], axis=1, keepdims=True)
        result = result.astype(jnp.bfloat16)
        for j in range(4):
            out[:, pl.ds(pl.multiple_of(i * 4 * HD + j * HD, HD), HD)] = result[j * SPAN : (j + 1) * SPAN]
        return carry

    lax.fori_loop(0, 2 * KVH, step, 0)


def attend_kernel(anc, lengths, q, kvn, pk, gbuf, out, m_ref, l_ref, acc_ref):
    dom, ctx = lax.axis_index("dom"), lax.axis_index("ctx")
    limit = lengths[anc[dom * PG + ctx]] * PAGE
    state = (m_ref, l_ref, acc_ref)
    absorb_new(q, kvn, state)
    for b in range(0, NY, 2):
        absorb_prompt(q, pk, state, (b, b + 1))
    absorb_pages(q, gbuf, limit, state)
    finish(state, out)


def attend(anc, lengths, q, kvn, pk, gbuf):
    vmem = pl.BlockSpec(memory_space=pltpu.VMEM)
    smem = pl.BlockSpec(memory_space=pltpu.SMEM)
    return pl.pallas_call(
        attend_kernel,
        out_shape=jax.ShapeDtypeStruct((SPAN, H * HD), jnp.bfloat16),
        in_specs=[smem, smem, vmem, vmem, vmem, vmem],
        out_specs=vmem,
        scratch_shapes=[pltpu.VMEM((2 * KVH, BLOCK, HD), jnp.float32)] * 3,
        compiler_params=pltpu.CompilerParams(vmem_limit_bytes=50 * 2**20),
        name="attend",
    )(anc, lengths, q, kvn, pk, gbuf)


def on_device(q_new, kv_new, prompt_kv, cache_kv, ancestors, lengths):
    prompt = prompt_kv.transpose(1, 0, 2)
    cache = cache_kv.transpose(0, 2, 1, 3).reshape(PG, ROWS, KVW)
    kvn = kv_new.transpose(1, 0, 2)
    pk, gbuf = exchange(ancestors, prompt, cache)
    return attend(ancestors, lengths, q_new, kvn, pk, gbuf)


def solution(mesh):
    placed = (
        P(("dom", "ctx"), None),
        P(("dom", "ctx"), None, None),
        P("ctx", None, None),
        P("dom", "ctx", None, None),
        P(),
        P(),
    )
    return jax.shard_map(
        on_device, mesh=mesh, in_specs=placed, out_specs=P(("dom", "ctx"), None), check_vma=False
    )
```

time: 231 us -> 103 us (0.45)
  the two profiles are of different devices: /device:TPU:6 before, /device:TPU:64 now
where the time goes in v1:
time: 103 us; the launch traced here: 102 us
  Pallas kernels  94.1 us (91%)
  local copies, waits for them, and re-layouts  8.2 us (8%)
    pallas_call x1, Pallas kernels, exchange(): pl.pallas_call(exchange_kernel, out_shape=(jax.ShapeDtypeStruct((2, NY, Z...  63.5 us
    pallas_call x1, Pallas kernels, attend(): pl.pallas_call(attend_kernel, out_shape=jax.ShapeDtypeStruct((SPAN, H * H...  30.6 us
    unnamed x12, local copies, waits for them, and re-layouts  7.09 us

profile of v1, /device:TPU:64, one launch (start us, length us, event | category | flops | bytes accessed | tf_op | source)
XLA Modules:
  0.0 102.4 jit_solution(5517909411622216438)
XLA Ops:
  0.0 0.9 copy.15
  0.9 1.0 copy.14
  1.9 1.1 %copy.13 = bf16[32,2,8,512]{3,2,1,0:T(8,128)(2,1)S(1)} copy(bf16[32,2,8,512]{3,1,2,0:T(2,128)(2,1)} %bitcast.13) | data formatting | bytes 1048576 | tf_op jit(solution)/shard_map/transpose | solution.py:335
  3.0 0.0 copy-start.2
  3.0 0.7 copy-done.2
  3.7 63.5 %exchange.1 = (bf16[2,8,256,512]{3,2,1,0:T(8,128)(2,1)S(1)}, bf16[32,16,512]{2,1,0:T(8,128)(2,1)S(1)}) custom-call(s32[512]{0:T(512)S(1)} %copy-done.2, bf16[2,64,512]{2,1,0:T(8,128)(2,1)S(1)} %bitcast.12, bf16[32,16,512]{2,1,0:T(8,128)(2,1)S(1)} %bitcast.10), custom_call_target="tpu_custom_call" | custom-call | tf_op jit(solution)/shard_map/exchange/pallas_call | solution.py:193
  67.2 0.0 copy-start
  67.2 1.9 %copy-done = bf16[2,8,256,512]{3,2,1,0:T(8,128)(2,1)} copy-done((bf16[2,8,256,512]{3,2,1,0:T(8,128)(2,1)}, bf16[2,8,256,512]{3,2,1,0:T(8,128)(2,1)S(1)}, u32[]{:S(2)}) %copy-start) | copy-done | bytes 4194328
  69.2 0.0 copy-start.1
  69.2 1.2 %copy-done.1 = bf16[128,4096]{1,0:T(8,128)(2,1)S(1)} copy-done((bf16[128,4096]{1,0:T(8,128)(2,1)S(1)}, bf16[128,4096]{1,0:T(8,128)(2,1)}, u32[]{:S(2)}) %copy-start.1) | copy-done | bytes 1048600
  70.4 0.0 copy-start.3
  70.4 0.7 copy-done.3
  71.1 0.0 copy-start.4
  71.1 0.7 copy-done.4
  71.7 30.6 %attend.1 = bf16[128,4096]{1,0:T(8,128)(2,1)} custom-call(s32[512]{0:T(512)S(1)} %copy-done.3, s32[512]{0:T(512)S(1)} %copy-done.4, bf16[128,4096]{1,0:T(8,128)(2,1)S(1)} %copy-done.1, bf16[2,128,512]{2,1,0:T(8,128)(2,1)S(1)} %bitcast.11, bf16[2,8,256,512]{3,2,1,0:T(8,128)(2,1)} %copy-done, bf16[32,16,512]{2,1,0:T(8,128)(2,1)S(1)} %get-tuple-element.8.gbuf), custom_call_target="tpu_custom_call" | custom-call | tf_op jit(solution)/shard_map/attend/pallas_call | solution.py:322
Async XLA Ops:
  3.0 0.7 copy-start.2
  67.2 1.9 %copy-start = (bf16[2,8,256,512]{3,2,1,0:T(8,128)(2,1)}, bf16[2,8,256,512]{3,2,1,0:T(8,128)(2,1)S(1)}, u32[]{:S(2)}) copy-start(bf16[2,8,256,512]{3,2,1,0:T(8,128)(2,1)S(1)} %get-tuple-element.7.pk) | copy-start | bytes 12582916
  69.2 1.2 %copy-start.1 = (bf16[128,4096]{1,0:T(8,128)(2,1)S(1)}, bf16[128,4096]{1,0:T(8,128)(2,1)}, u32[]{:S(2)}) copy-start(bf16[128,4096]{1,0:T(8,128)(2,1)} %q.1) | copy-start | bytes 3145732
  70.4 0.7 copy-start.3
  71.1 0.7 copy-start.4

commit v2 on v1

v2 whole, which is shorter than its diff:
```python
import functools

import jax
import jax.numpy as jnp
from jax import lax
from jax.experimental import pallas as pl
from jax.experimental.pallas import tpu as pltpu
from jax.sharding import PartitionSpec as P

HD = 128
H = 32
KVH = 4
SPAN = 128
PAGE = 8
GQ = 8
NDOM = 16
NCTX = 32
NY = 8
NZLO = 4
PG = 32
CAP = 4
SHARD = 64
ZBLOCK = SHARD * NZLO
KVW = KVH * HD
ROWS = 2 * PAGE
RUN = CAP * ROWS
NEGATIVE = -1e30
SCALE = HD ** (-0.5) * 1.4426950408889634


def place():
    dom = lax.axis_index("dom")
    ctx = lax.axis_index("ctx")
    core = dom % 2
    z_hi = (dom // 2) % 2
    x = dom // 4
    z_lo = ctx // NY
    y = ctx % NY
    return dom, ctx, x, z_hi, core, z_lo, y


def at_z(x, core, y, z):
    z = z % (2 * NZLO)
    return {"dom": (x * 2 + z // NZLO) * 2 + core, "ctx": (z % NZLO) * NY + y}


def rcopy(src, dst, send, recv, target):
    return pltpu.make_async_remote_copy(
        src_ref=src,
        dst_ref=dst,
        send_sem=send,
        recv_sem=recv,
        device_id=target,
        device_id_type=pl.DeviceIdType.MESH,
    )


def attend_kernel(
    anc_hbm, len_hbm, prompt, cache, q_hbm, kvn, out_hbm,
    anc, lens, q, out, pk, abuf, bbuf, ybuf, gbuf, m_ref, l_ref, acc_ref,
    ar0, ar1, ar2, ar3, br0, br1, br2, br3, in_sem, z_send, z_recv, r_send, r_recv, l_send, l_recv, c_send, c_recv,
    a_send, a_recv, b_send, b_recv, p_send, p_recv, out_sem,
):
    dom, ctx, x, z_hi, core, z_lo, y = place()
    z = z_hi * NZLO + z_lo
    e = x * 2 + core
    sibling = {"dom": dom + 1 - 2 * core, "ctx": ctx}
    right = {"dom": dom, "ctx": z_lo * NY + (y + 1) % NY}
    left = {"dom": dom, "ctx": z_lo * NY + (y + NY - 1) % NY}
    state = (m_ref, l_ref, acc_ref)
    arecv, brecv = (ar0, ar1, ar2, ar3), (br0, br1, br2, br3)

    def at_e(o):
        other = (e + o) % NY
        return {"dom": ((other // 2) * 2 + z_hi) * 2 + other % 2, "ctx": ctx}

    def at_y(o):
        return {"dom": dom, "ctx": z_lo * NY + (y + o) % NY}

    barrier = pltpu.get_barrier_semaphore()
    fetch = [
        pltpu.make_async_copy(anc_hbm, anc, in_sem.at[0]),
        pltpu.make_async_copy(len_hbm, lens, in_sem.at[1]),
        pltpu.make_async_copy(q_hbm, q, in_sem.at[2]),
    ]
    for copy in fetch:
        copy.start()
    for o in range(1, NY):
        for target in (at_e(o), at_z(x, core, y, z + o), at_y(o)):
            pl.semaphore_signal(barrier, inc=1, device_id=target, device_id_type=pl.DeviceIdType.MESH)
    own_rows = pl.ds(z_lo * SHARD, SHARD)
    pk[core, y, own_rows, :] = prompt[core]
    fetch[0].wait()
    fetch[1].wait()

    def pick_first(d, carry):
        run = 0
        for r in range(PG // CAP):
            run = jnp.where(anc[d * PG + r * CAP] // PG == dom, r, run)
        for k in range(CAP):
            page = cache[anc[d * PG + run * CAP + k] % PG]
            for g in range(KVH):
                abuf[g, (d // 4) * 2 + d % 2, (d // 2) % 2, k * ROWS : (k + 1) * ROWS, :] = page[
                    :, g * HD : (g + 1) * HD
                ]
        return carry

    lax.fori_loop(0, NDOM, pick_first, 0)
    pl.semaphore_wait(barrier, 3 * (NY - 1))

    far = 2 - 4 * (z % 2)
    z_copies = [
        rcopy(pk.at[core, y, own_rows], pk.at[core, y, own_rows], z_send.at[i], z_recv.at[i],
              at_z(x, core, y, z + hop + 8))
        for i, hop in enumerate((1, -1, far))
    ]
    for copy in z_copies:
        copy.start()

    def a_copy(g, o):
        return rcopy(abuf.at[g, (e + o) % NY], arecv[g].at[e], a_send.at[g, o], a_recv.at[g, o], at_e(o))

    def b_copy(g, o):
        return rcopy(bbuf.at[g, (z + o) % NY], brecv[g].at[z], b_send.at[g, o], b_recv.at[g, o],
                     at_z(x, core, y, z + o))

    def p_copy(g, o):
        return rcopy(ybuf.at[g, (y + o) % NY], gbuf.at[g, y], p_send.at[g, o], p_recv.at[g, o], at_y(o))

    def start_all(make, g):
        for o in range(1, NY):
            make(g, o).start()

    def wait_all(make, g):
        for o in range(1, NY):
            make(g, o).wait()

    for g in range(KVH):
        start_all(a_copy, g)
        arecv[g][e] = abuf[g, e]

    def along_z(g):
        wait_all(a_copy, g)

        def pick(zz, carry):
            to_hi = zz // NZLO
            for j in range(2):
                source = anc[(x * 4 + to_hi * 2 + core) * PG + (zz % NZLO) * 8 + j * CAP] // PG
                bbuf[g, zz, j] = arecv[g][(source // 4) * 2 + source % 2, to_hi]
            return carry

        lax.fori_loop(0, NY, pick, 0)
        start_all(b_copy, g)
        brecv[g][z] = bbuf[g, z]

    def along_y(g):
        wait_all(b_copy, g)
        for j in range(2):
            source = anc[dom * PG + z_lo * 8 + j * CAP] // PG
            for zl in range(NZLO):
                pages = brecv[g][((source // 2) % 2) * NZLO + zl, j]
                for k in range(CAP):
                    ybuf[g, j * CAP + k, zl * ROWS : (zl + 1) * ROWS, :] = pages[k * ROWS : (k + 1) * ROWS]
        start_all(p_copy, g)
        gbuf[g, y] = ybuf[g, y]

    def core_copy(i, yy):
        return rcopy(pk.at[core, yy], pk.at[core, yy], c_send.at[i], c_recv.at[i], sibling)

    half = ZBLOCK // 2
    rights, lefts, cores = [], [], []

    def ring_step(t):
        yr = (y + NY - t) % NY
        yl = (y + t) % NY
        if t == 0:
            for copy in z_copies:
                copy.wait()
        else:
            rights[t - 1].wait_recv()
            lefts[t - 1].wait_recv()
        if t < 4:
            rrows = pl.ds(0, ZBLOCK if t < 3 else half)
            lrows = pl.ds(0 if t < 3 else half, ZBLOCK if t < 3 else half)
            rights.append(
                rcopy(pk.at[core, yr, rrows], pk.at[core, yr, rrows], r_send.at[t], r_recv.at[t], right)
            )
            lefts.append(
                rcopy(pk.at[core, yl, lrows], pk.at[core, yl, lrows], l_send.at[t], l_recv.at[t], left)
            )
            rights[t].start()
            lefts[t].start()
        for i, yy in ((0, y),) if t == 0 else ((7, yr),) if t == 4 else ((2 * t - 1, yr), (2 * t, yl)):
            cores.append(core_copy(i, yy))
            cores[-1].start()

    def prompt_part(t, begin, end):
        yr = (y + NY - t) % NY
        yl = (y + t) % NY
        absorb_prompt(q, pk, state, (yr,) if t in (0, 4) else (yr, yl), begin, end)

    def await_cores(t):
        for copy in cores[0:1] if t == 0 else cores[7:8] if t == 4 else cores[2 * t - 1 : 2 * t + 1]:
            copy.wait()

    fetch[2].wait()
    ring_step(0)
    absorb_new(q, kvn, state)
    along_z(0)
    await_cores(0)
    prompt_part(0, 0, 4)
    along_z(1)
    ring_step(1)
    await_cores(1)
    prompt_part(1, 0, 2)
    along_z(2)
    along_y(0)
    prompt_part(1, 2, 4)
    along_z(3)
    ring_step(2)
    await_cores(2)
    prompt_part(2, 0, 2)
    along_y(1)
    prompt_part(2, 2, 4)
    ring_step(3)
    await_cores(3)
    prompt_part(3, 0, 2)
    along_y(2)
    prompt_part(3, 2, 4)
    ring_step(4)
    along_y(3)
    await_cores(4)
    prompt_part(4, 0, 4)
    limit = lens[anc[dom * PG + ctx]]
    outs = []
    for g in range(KVH):
        wait_all(p_copy, g)
        absorb_pages(q, gbuf, limit, state, g)
        finish(state, out, g)
        cols = pl.ds(g * GQ * HD, GQ * HD)
        outs.append(pltpu.make_async_copy(out.at[:, cols], out_hbm.at[:, cols], out_sem.at[g]))
        outs[-1].start()
    for t in range(4):
        rights[t].wait_send()
        lefts[t].wait_send()
    for copy in outs:
        copy.wait()


BLOCK = GQ * SPAN


def queries_of(q, g):
    return jnp.concatenate(
        [q[:, pl.ds(pl.multiple_of(g * BLOCK + j * HD, HD), HD)] for j in range(GQ)], axis=0
    )


def absorb(q, state, g, keys, values, visible, first):
    m_ref, l_ref, acc_ref = state
    n = keys.shape[0]
    scores = lax.dot_general(
        queries_of(q, g), keys, (((1,), (1,)), ((), ())), preferred_element_type=jnp.float32
    )
    if visible is not None:
        scores = jnp.where(visible, scores, NEGATIVE)
    top = scores[:, :HD]
    for i in range(1, n // HD):
        top = jnp.maximum(top, scores[:, i * HD : (i + 1) * HD])
    if not first:
        m_old = m_ref[g]
        top = jnp.maximum(top, m_old)
    m_new = jnp.broadcast_to(jnp.max(top, axis=1, keepdims=True), (BLOCK, HD))
    weights = [jnp.exp2((scores[:, i * HD : (i + 1) * HD] - m_new) * SCALE) for i in range(n // HD)]
    total = weights[0]
    for part in weights[1:]:
        total = total + part
    weights = jnp.concatenate(weights, axis=1)
    added = jnp.dot(weights.astype(jnp.bfloat16), values, preferred_element_type=jnp.float32)
    if first:
        l_ref[g] = total
        acc_ref[g] = added
    else:
        factor = jnp.exp2((m_old - m_new) * SCALE)
        l_ref[g] = factor * l_ref[g] + total
        acc_ref[g] = factor * acc_ref[g] + added
    m_ref[g] = m_new


def head_cols(g):
    return pl.ds(pl.multiple_of(g * HD, HD), HD)


def absorb_new(q, kvn, state):
    def step(g, carry):
        cols = head_cols(g)
        row = lax.broadcasted_iota(jnp.int32, (BLOCK, SPAN), 0) % SPAN
        col = lax.broadcasted_iota(jnp.int32, (BLOCK, SPAN), 1)
        absorb(q, state, g, kvn[0, :, cols], kvn[1, :, cols], col <= row, True)
        return carry

    lax.fori_loop(0, KVH, step, 0)


def absorb_prompt(q, pk, state, blocks, begin, end):
    def step(g, carry):
        cols = head_cols(g)
        keys = jnp.concatenate([pk[0, b, :, cols] for b in blocks], axis=0)
        values = jnp.concatenate([pk[1, b, :, cols] for b in blocks], axis=0)
        absorb(q, state, g, keys, values, None, False)
        return carry

    lax.fori_loop(begin, end, step, 0)


def absorb_pages(q, gbuf, limit, state, g):
    pages = gbuf[g].reshape(NCTX, ROWS, HD).astype(jnp.float32)
    keys = pages[:, :PAGE].reshape(NCTX * PAGE, HD).astype(jnp.bfloat16)
    values = pages[:, PAGE:].reshape(NCTX * PAGE, HD).astype(jnp.bfloat16)
    slot = lax.broadcasted_iota(jnp.int32, (BLOCK, NCTX * PAGE), 1) // PAGE
    page = (slot % NZLO) * NY + slot // NZLO
    absorb(q, state, g, keys, values, page < limit, False)


def finish(state, out, g):
    m_ref, l_ref, acc_ref = state
    result = acc_ref[g] / jnp.sum(l_ref[g], axis=1, keepdims=True)
    result = result.astype(jnp.bfloat16)
    for j in range(GQ):
        out[:, g * BLOCK + j * HD : g * BLOCK + (j + 1) * HD] = result[j * SPAN : (j + 1) * SPAN]


def attend(anc, lengths, prompt, cache, q, kvn):
    vmem = pl.BlockSpec(memory_space=pltpu.VMEM)
    hbm = pl.BlockSpec(memory_space=pltpu.HBM)
    dma = pltpu.SemaphoreType.DMA
    bf16 = jnp.bfloat16
    return pl.pallas_call(
        attend_kernel,
        out_shape=jax.ShapeDtypeStruct((SPAN, H * HD), bf16),
        in_specs=[hbm, hbm, vmem, vmem, hbm, vmem],
        out_specs=hbm,
        scratch_shapes=[
            pltpu.SMEM((PG * NDOM,), jnp.int32),
            pltpu.SMEM((PG * NDOM,), jnp.int32),
            pltpu.VMEM((SPAN, H * HD), bf16),
            pltpu.VMEM((SPAN, H * HD), bf16),
            pltpu.VMEM((2, NY, ZBLOCK, KVW), bf16),
            pltpu.VMEM((KVH, 8, 2, RUN, HD), bf16),
            pltpu.VMEM((KVH, 8, 2, RUN, HD), bf16),
            pltpu.VMEM((KVH, NY, RUN, HD), bf16),
            pltpu.VMEM((KVH, NY, RUN, HD), bf16),
        ]
        + [pltpu.VMEM((KVH, BLOCK, HD), jnp.float32)] * 3
        + [pltpu.VMEM((8, 2, RUN, HD), bf16)] * (2 * KVH)
        + [
            dma((3,)), dma((3,)), dma((3,)), dma((4,)), dma((4,)), dma((4,)), dma((4,)),
            dma((8,)), dma((8,)),
        ]
        + [dma((KVH, 8))] * 6
        + [dma((KVH,))],
        compiler_params=pltpu.CompilerParams(
            collective_id=0, has_side_effects=True, vmem_limit_bytes=50 * 2**20
        ),
        name="attend",
    )(anc, lengths, prompt, cache, q, kvn)


def on_device(q_new, kv_new, prompt_kv, cache_kv, ancestors, lengths):
    prompt = prompt_kv.transpose(1, 0, 2)
    cache = cache_kv.transpose(0, 2, 1, 3).reshape(PG, ROWS, KVW)
    kvn = kv_new.transpose(1, 0, 2)
    return attend(ancestors, lengths, prompt, cache, q_new, kvn)


def solution(mesh):
    placed = (
        P(("dom", "ctx"), None),
        P(("dom", "ctx"), None, None),
        P("ctx", None, None),
        P("dom", "ctx", None, None),
        P(),
        P(),
    )
    return jax.shard_map(
        on_device, mesh=mesh, in_specs=placed, out_specs=P(("dom", "ctx"), None), check_vma=False
    )
```

time: 103 us -> 65.6 us (0.64)
  the two profiles are of different devices: /device:TPU:64 before, /device:TPU:1 now
where the time goes in v2:
time: 65.6 us; the launch traced here: 65.5 us
  Pallas kernels  61.7 us (94%)
  local copies, waits for them, and re-layouts  3.66 us (6%)
    pallas_call x1, Pallas kernels, attend(): pl.pallas_call(attend_kernel, out_shape=jax.ShapeDtypeStruct((SPAN, H * H...  61.7 us
    unnamed x11, local copies, waits for them, and re-layouts  3.6 us

profile of v2, /device:TPU:1, one launch (start us, length us, event | category | flops | bytes accessed | tf_op | source)
XLA Modules:
  0.0 65.5 jit_solution(15379985256453679872)
XLA Ops:
  0.0 0.0 copy-start.3
  0.0 0.0 copy-start
  0.0 1.0 %copy.15 = bf16[64,2,512]{2,0,1:T(8,128)(2,1)S(1)} copy(bf16[64,2,512]{2,1,0:T(2,128)(2,1)} %param.8) | data formatting | bytes 262144 | tf_op args[2]
  1.0 1.0 %copy.14 = bf16[128,2,512]{2,0,1:T(8,128)(2,1)S(1)} copy(bf16[128,2,512]{2,1,0:T(2,128)(2,1)} %param.7) | data formatting | bytes 524288 | tf_op args[1]
  2.0 0.0 copy-done.3
  2.0 0.0 copy-start.1
  2.1 0.0 copy-start.2
  2.1 0.1 copy.13
  2.1 0.0 copy-done
  2.1 0.6 copy-done.1
  2.7 0.0 copy-done.2
  2.7 61.7 %attend.1 = bf16[128,4096]{1,0:T(8,128)(2,1)S(1)} custom-call(s32[512]{0:T(512)S(1)} %copy-done.1, s32[512]{0:T(512)S(1)} %copy-done.2, bf16[2,64,512]{2,1,0:T(8,128)(2,1)S(1)} %bitcast.12, bf16[32,16,512]{2,1,0:T(8,128)(2,1)S(1)} %bitcast.10, bf16[128,4096]{1,0:T(8,128)(2,1)S(1)} %copy-done, bf16[2,128,512]{2,1,0:T(8,128)(2,1)S(1)} %bitcast.11), custom_call_target="tpu_custom_call" | custom-call | tf_op jit(solution)/shard_map/attend/pallas_call | solution.py:338
  64.5 1.0 %copy.17 = bf16[128,4096]{1,0:T(8,128)(2,1)} copy(bf16[128,4096]{1,0:T(8,128)(2,1)S(1)} %attend.1) | data formatting | bytes 2097152
Async XLA Ops:
  0.0 2.0 %copy-start.3 = (bf16[32,8,2,512]{3,2,1,0:T(2,128)(2,1)S(1)}, bf16[32,8,2,512]{3,2,1,0:T(2,128)(2,1)}, u32[]{:S(2)}) copy-start(bf16[32,8,2,512]{3,2,1,0:T(2,128)(2,1)} %param.9) | copy-start | bytes 1572868
  0.0 2.1 %copy-start = (bf16[128,4096]{1,0:T(8,128)(2,1)S(1)}, bf16[128,4096]{1,0:T(8,128)(2,1)}, u32[]{:S(2)}) copy-start(bf16[128,4096]{1,0:T(8,128)(2,1)} %q_hbm.1) | copy-start | bytes 3145732
  2.0 0.7 %copy-start.1 = (s32[512]{0:T(512)S(1)}, s32[512]{0:T(512)}, u32[]{:S(2)}) copy-start(s32[512]{0:T(512)} %anc_hbm.1) | copy-start | bytes 6148
  2.1 0.7 %copy-start.2 = (s32[512]{0:T(512)S(1)}, s32[512]{0:T(512)}, u32[]{:S(2)}) copy-start(s32[512]{0:T(512)} %len_hbm.1) | copy-start | bytes 6148

commit v3 on v2

v3 whole, which is shorter than its diff:
```python
import functools

import jax
import jax.numpy as jnp
from jax import lax
from jax.experimental import pallas as pl
from jax.experimental.pallas import tpu as pltpu
from jax.sharding import PartitionSpec as P

HD = 128
H = 32
KVH = 4
SPAN = 128
PAGE = 8
GQ = 8
NDOM = 16
NCTX = 32
NY = 8
NZLO = 4
PG = 32
CAP = 4
SHARD = 64
ZBLOCK = SHARD * NZLO
KVW = KVH * HD
ROWS = 2 * PAGE
RUN = CAP * ROWS
FAR_FIRST = (4, 3, 5, 2, 6, 1, 7)
NEGATIVE = -1e30
SCALE = HD ** (-0.5) * 1.4426950408889634


def place():
    dom = lax.axis_index("dom")
    ctx = lax.axis_index("ctx")
    core = dom % 2
    z_hi = (dom // 2) % 2
    x = dom // 4
    z_lo = ctx // NY
    y = ctx % NY
    return dom, ctx, x, z_hi, core, z_lo, y


def at_z(x, core, y, z):
    z = z % (2 * NZLO)
    return {"dom": (x * 2 + z // NZLO) * 2 + core, "ctx": (z % NZLO) * NY + y}


def rcopy(src, dst, send, recv, target):
    return pltpu.make_async_remote_copy(
        src_ref=src,
        dst_ref=dst,
        send_sem=send,
        recv_sem=recv,
        device_id=target,
        device_id_type=pl.DeviceIdType.MESH,
    )


def attend_kernel(
    anc_hbm, len_hbm, prompt_hbm, cache_hbm, q_hbm, kvn_hbm, out_hbm,
    anc, lens, local, cache_raw, cache, prompt, kvn_raw, kvn, q, out, pk, abuf, bbuf, ybuf, gbuf, m_ref, l_ref, acc_ref,
    ar0, ar1, ar2, ar3, br0, br1, br2, br3, in_sem,
    z_send, z_recv, r_send, r_recv, l_send, l_recv, c_send, c_recv,
    a_send, a_recv, b_send, b_recv, p_send, p_recv, out_sem,
):
    dom, ctx, x, z_hi, core, z_lo, y = place()
    z = z_hi * NZLO + z_lo
    e = x * 2 + core
    sibling = {"dom": dom + 1 - 2 * core, "ctx": ctx}
    right = {"dom": dom, "ctx": z_lo * NY + (y + 1) % NY}
    left = {"dom": dom, "ctx": z_lo * NY + (y + NY - 1) % NY}
    state = (m_ref, l_ref, acc_ref)
    arecv, brecv = (ar0, ar1, ar2, ar3), (br0, br1, br2, br3)

    def at_e(o):
        other = (e + o) % NY
        return {"dom": ((other // 2) * 2 + z_hi) * 2 + other % 2, "ctx": ctx}

    def at_y(o):
        return {"dom": dom, "ctx": z_lo * NY + (y + o) % NY}

    barrier = pltpu.get_barrier_semaphore()
    fetch = [
        pltpu.make_async_copy(anc_hbm, anc, in_sem.at[0]),
        pltpu.make_async_copy(prompt_hbm, prompt, in_sem.at[1]),
        pltpu.make_async_copy(cache_hbm, cache_raw, in_sem.at[5]),
        pltpu.make_async_copy(len_hbm, lens, in_sem.at[2]),
        pltpu.make_async_copy(kvn_hbm, kvn_raw, in_sem.at[3]),
        pltpu.make_async_copy(q_hbm, q, in_sem.at[4]),
    ]
    for copy in fetch:
        copy.start()
    for o in range(1, NY):
        for target in (at_e(o), at_z(x, core, y, z + o), at_y(o)):
            pl.semaphore_signal(barrier, inc=1, device_id=target, device_id_type=pl.DeviceIdType.MESH)
    own_rows = pl.ds(z_lo * SHARD, SHARD)
    fetch[1].wait()
    both = jnp.swapaxes(prompt[...], 0, 1)
    pk[core, y, own_rows, :] = jnp.where(core == 0, both[0], both[1])
    pl.semaphore_wait(barrier, 3 * (NY - 1))

    far = 2 - 4 * (z % 2)
    z_copies = [
        rcopy(pk.at[core, y, own_rows], pk.at[core, y, own_rows], z_send.at[i], z_recv.at[i],
              at_z(x, core, y, z + hop + 8))
        for i, hop in enumerate((far, 1, -1))
    ]
    for copy in z_copies:
        copy.start()

    fetch[0].wait()

    def choose(d, carry):
        run = 0
        for r in range(PG // CAP):
            run = jnp.where(anc[d * PG + r * CAP] // PG == dom, r, run)
        for k in range(CAP):
            local[d * CAP + k] = anc[d * PG + run * CAP + k] % PG
        return carry

    lax.fori_loop(0, NDOM, choose, 0, unroll=4)

    def pick_first(g):
        pages = jnp.swapaxes(cache_raw[:, :, :, g * HD : (g + 1) * HD], 1, 2)
        cache[g] = pages.reshape(PG, ROWS, HD)

        def pick(d, carry):
            for k in range(CAP):
                abuf[g, (d // 4) * 2 + d % 2, (d // 2) % 2, k * ROWS : (k + 1) * ROWS, :] = cache[
                    g, local[d * CAP + k]
                ]
            return carry

        lax.fori_loop(0, NDOM, pick, 0, unroll=4)

    fetch[2].wait()
    pick_first(0)
    def a_copy(g, o):
        return rcopy(abuf.at[g, (e + o) % NY], arecv[g].at[e], a_send.at[g, o], a_recv.at[g, o], at_e(o))

    def b_copy(g, o):
        return rcopy(bbuf.at[g, (z + o) % NY], brecv[g].at[z], b_send.at[g, o], b_recv.at[g, o],
                     at_z(x, core, y, z + o))

    def p_copy(g, o):
        return rcopy(ybuf.at[g, (y + o) % NY], gbuf.at[g, y], p_send.at[g, o], p_recv.at[g, o], at_y(o))

    def start_all(make, g):
        for o in FAR_FIRST:
            make(g, o).start()

    def wait_all(make, g):
        for o in FAR_FIRST:
            make(g, o).wait()

    def along_x(g):
        if g > 0:
            pick_first(g)
        start_all(a_copy, g)
        arecv[g][e] = abuf[g, e]

    def along_z(g):
        wait_all(a_copy, g)

        def pick(zz, carry):
            to_hi = zz // NZLO
            for j in range(2):
                source = anc[(x * 4 + to_hi * 2 + core) * PG + (zz % NZLO) * 8 + j * CAP] // PG
                bbuf[g, zz, j] = arecv[g][(source // 4) * 2 + source % 2, to_hi]
            return carry

        lax.fori_loop(0, NY, pick, 0, unroll=4)
        start_all(b_copy, g)
        brecv[g][z] = bbuf[g, z]

    def along_y(g):
        wait_all(b_copy, g)
        for j in range(2):
            source = anc[dom * PG + z_lo * 8 + j * CAP] // PG
            for zl in range(NZLO):
                pages = brecv[g][((source // 2) % 2) * NZLO + zl, j]
                for k in range(CAP):
                    ybuf[g, j * CAP + k, zl * ROWS : (zl + 1) * ROWS, :] = pages[k * ROWS : (k + 1) * ROWS]
        start_all(p_copy, g)
        gbuf[g, y] = ybuf[g, y]

    half = ZBLOCK // 2

    def piece(yy, p):
        return pk.at[core, yy, pl.ds(p * half, half)]

    def hop_copy(t, p, to_right):
        yy = (y + NY - t) % NY if to_right else (y + t) % NY
        send, recv = (r_send, r_recv) if to_right else (l_send, l_recv)
        return rcopy(piece(yy, p), piece(yy, p), send.at[t, p], recv.at[t, p], right if to_right else left)

    def core_copy(t, p, to_right):
        yy = (y + NY - t) % NY if to_right else (y + t) % NY
        i = t if to_right else NY - t
        return rcopy(piece(yy, p), piece(yy, p), c_send.at[i, p], c_recv.at[i, p], sibling)

    def sides(t, p):
        return (True,) if t == 0 or (t == 4 and p == 0) else (False,) if t == 4 else (True, False)

    def ring_step(t, p):
        if t == 0 and p == 0:
            for copy in z_copies:
                copy.wait()
        for side in sides(t, p):
            if t > 0:
                hop_copy(t - 1, p, side).wait_recv()
            if t < 3 or (t == 3 and side == (p == 0)):
                hop_copy(t, p, side).start()
                if t == 0:
                    hop_copy(t, p, False).start()
            core_copy(t, p, side).start()

    def near_part(g, carry):
        absorb_near(q, pk, kvn, state, y, g)
        return carry

    def await_cores(t):
        for p in range(2):
            for side in sides(t, p):
                core_copy(t, p, side).wait()

    along_x(0)
    along_x(1)
    along_x(2)
    along_x(3)
    along_z(0)
    ring_step(0, 0)
    ring_step(0, 1)
    along_z(1)
    for copy in fetch[3:]:
        copy.wait()
    kvn[...] = jnp.swapaxes(kvn_raw[...], 0, 1)
    await_cores(0)
    lax.fori_loop(0, KVH, near_part, 0)
    along_z(2)
    ring_step(1, 0)
    ring_step(1, 1)
    along_z(3)
    await_cores(1)

    def ring_part(i, carry):
        @pl.when(i == 1)
        def _():
            along_y(0)

        @pl.when(i == 4)
        def _():
            ring_step(2, 0)
            ring_step(2, 1)
            await_cores(2)

        @pl.when(i == 5)
        def _():
            along_y(1)

        @pl.when(i == 8)
        def _():
            ring_step(3, 0)
            ring_step(3, 1)
            await_cores(3)

        @pl.when(i == 9)
        def _():
            along_y(2)

        @pl.when(i == 11)
        def _():
            along_y(3)

        absorb_ring(q, pk, state, y, 1 + i // KVH, i % KVH)
        return carry

    lax.fori_loop(0, 3 * KVH, ring_part, 0)
    ring_step(4, 0)
    ring_step(4, 1)
    await_cores(4)
    limit = lens[anc[dom * PG + ctx]]

    def out_copy(g):
        cols = pl.ds(pl.multiple_of(g * BLOCK, BLOCK), BLOCK)
        return pltpu.make_async_copy(out.at[:, cols], out_hbm.at[:, cols], out_sem.at[g])

    def last_part(g, carry):
        wait_all(p_copy, g)
        absorb_last(q, pk, gbuf, limit, state, y, g)
        finish(state, out, g)
        out_copy(g).start()
        return carry

    lax.fori_loop(0, KVH, last_part, 0)
    for t in range(4):
        for p in range(2):
            for side in (True, False):
                if t < 3 or side == (p == 0):
                    hop_copy(t, p, side).wait_send()
    for g in range(KVH):
        out_copy(g).wait()


BLOCK = GQ * SPAN


def queries_of(q, g):
    return jnp.concatenate(
        [q[:, pl.ds(pl.multiple_of(g * BLOCK + j * HD, HD), HD)] for j in range(GQ)], axis=0
    )


def absorb(q, state, g, keys, values, masks, first):
    m_ref, l_ref, acc_ref = state
    scores = lax.dot_general(
        queries_of(q, g), keys, (((1,), (1,)), ((), ())), preferred_element_type=jnp.float32
    )
    tiles = [scores[:, i * HD : (i + 1) * HD] for i in range(keys.shape[0] // HD)]
    for i, visible in masks:
        tiles[i] = jnp.where(visible, tiles[i], NEGATIVE)
    top = functools.reduce(jnp.maximum, tiles)
    if not first:
        m_old = m_ref[g]
        top = jnp.maximum(top, m_old)
    m_new = jnp.broadcast_to(jnp.max(top, axis=1, keepdims=True), (BLOCK, HD))
    weights = [jnp.exp2((tile - m_new) * SCALE) for tile in tiles]
    total = functools.reduce(jnp.add, weights)
    weights = jnp.concatenate(weights, axis=1)
    added = jnp.dot(weights.astype(jnp.bfloat16), values, preferred_element_type=jnp.float32)
    if first:
        l_ref[g] = total
        acc_ref[g] = added
    else:
        factor = jnp.exp2((m_old - m_new) * SCALE)
        l_ref[g] = factor * l_ref[g] + total
        acc_ref[g] = factor * acc_ref[g] + added
    m_ref[g] = m_new


def head_cols(g):
    return pl.ds(pl.multiple_of(g * HD, HD), HD)


def absorb_near(q, pk, kvn, state, y, g):
    cols = head_cols(g)
    row = lax.broadcasted_iota(jnp.int32, (BLOCK, SPAN), 0) % SPAN
    col = lax.broadcasted_iota(jnp.int32, (BLOCK, SPAN), 1)
    keys = jnp.concatenate([pk[0, y, :, cols], kvn[0, :, cols]], axis=0)
    values = jnp.concatenate([pk[1, y, :, cols], kvn[1, :, cols]], axis=0)
    absorb(q, state, g, keys, values, [(ZBLOCK // HD, col <= row)], True)


def absorb_ring(q, pk, state, y, t, g):
    cols = head_cols(g)
    blocks = ((y + NY - t) % NY, (y + t) % NY)
    keys = jnp.concatenate([pk[0, b, :, cols] for b in blocks], axis=0)
    values = jnp.concatenate([pk[1, b, :, cols] for b in blocks], axis=0)
    absorb(q, state, g, keys, values, [], False)


def absorb_last(q, pk, gbuf, limit, state, y, g):
    cols = head_cols(g)
    far = (y + NY // 2) % NY
    pages = gbuf[g].reshape(NCTX, ROWS, HD).astype(jnp.float32)
    page_keys = pages[:, :PAGE].reshape(NCTX * PAGE, HD).astype(jnp.bfloat16)
    page_values = pages[:, PAGE:].reshape(NCTX * PAGE, HD).astype(jnp.bfloat16)
    keys = jnp.concatenate([pk[0, far, :, cols], page_keys], axis=0)
    values = jnp.concatenate([pk[1, far, :, cols], page_values], axis=0)
    masks = []
    for i in range(NCTX * PAGE // HD):
        slot = (lax.broadcasted_iota(jnp.int32, (BLOCK, HD), 1) + i * HD) // PAGE
        page = (slot % NZLO) * NY + slot // NZLO
        masks.append((ZBLOCK // HD + i, page < limit))
    absorb(q, state, g, keys, values, masks, False)


def finish(state, out, g):
    m_ref, l_ref, acc_ref = state
    result = acc_ref[g] / jnp.sum(l_ref[g], axis=1, keepdims=True)
    result = result.astype(jnp.bfloat16)
    for j in range(GQ):
        out[:, pl.ds(pl.multiple_of(g * BLOCK + j * HD, HD), HD)] = result[j * SPAN : (j + 1) * SPAN]


def attend(anc, lengths, prompt, cache, q, kvn):
    hbm = pl.BlockSpec(memory_space=pltpu.HBM)
    dma = pltpu.SemaphoreType.DMA
    bf16 = jnp.bfloat16
    return pl.pallas_call(
        attend_kernel,
        out_shape=jax.ShapeDtypeStruct((SPAN, H * HD), bf16),
        in_specs=[hbm] * 6,
        out_specs=hbm,
        scratch_shapes=[
            pltpu.SMEM((PG * NDOM,), jnp.int32),
            pltpu.SMEM((PG * NDOM,), jnp.int32),
            pltpu.SMEM((CAP * NDOM,), jnp.int32),
            pltpu.VMEM((PG, PAGE, 2, KVW), bf16),
            pltpu.VMEM((KVH, PG, ROWS, HD), bf16),
            pltpu.VMEM((SHARD, 2, KVW), bf16),
            pltpu.VMEM((SPAN, 2, KVW), bf16),
            pltpu.VMEM((2, SPAN, KVW), bf16),
            pltpu.VMEM((SPAN, H * HD), bf16),
            pltpu.VMEM((SPAN, H * HD), bf16),
            pltpu.VMEM((2, NY, ZBLOCK, KVW), bf16),
            pltpu.VMEM((KVH, 8, 2, RUN, HD), bf16),
            pltpu.VMEM((KVH, 8, 2, RUN, HD), bf16),
            pltpu.VMEM((KVH, NY, RUN, HD), bf16),
            pltpu.VMEM((KVH, NY, RUN, HD), bf16),
        ]
        + [pltpu.VMEM((KVH, BLOCK, HD), jnp.float32)] * 3
        + [pltpu.VMEM((8, 2, RUN, HD), bf16)] * (2 * KVH)
        + [
            dma((6,)), dma((3,)), dma((3,)), dma((4, 2)), dma((4, 2)), dma((4, 2)), dma((4, 2)),
            dma((8, 2)), dma((8, 2)),
        ]
        + [dma((KVH, 8))] * 6
        + [dma((KVH,))],
        compiler_params=pltpu.CompilerParams(
            collective_id=0, has_side_effects=True, vmem_limit_bytes=50 * 2**20
        ),
        name="attend",
    )(anc, lengths, prompt, cache, q, kvn)


def on_device(q_new, kv_new, prompt_kv, cache_kv, ancestors, lengths):
    args = (ancestors, lengths, prompt_kv, cache_kv, q_new, kv_new)
    return attend(*[pltpu.with_memory_space_constraint(a, pltpu.HBM) for a in args])


def solution(mesh):
    placed = (
        P(("dom", "ctx"), None),
        P(("dom", "ctx"), None, None),
        P("ctx", None, None),
        P("dom", "ctx", None, None),
        P(),
        P(),
    )
    return jax.shard_map(
        on_device, mesh=mesh, in_specs=placed, out_specs=P(("dom", "ctx"), None), check_vma=False
    )
```

time: 65.6 us -> 60.8 us (0.927)
  local copies, waits for them, and re-layouts: 3.66 us -> 0.97 us
  Pallas kernels: 61.7 us -> 59.7 us
    unnamed x11 -> x1, local copies, waits for them, and re-layouts: 3.6 us -> 0.97 us
    pallas_call x1, Pallas kernels: 61.7 us -> 59.7 us  [attend(): pl.pallas_call(attend_kernel, out_shape=jax.ShapeDtypeStruct((SPAN, H * H...]
where the time goes in v3:
time: 60.8 us; the launch traced here: 60.6 us
  Pallas kernels  59.7 us (98%)
  local copies, waits for them, and re-layouts  0.97 us (2%)
    pallas_call x1, Pallas kernels, attend(): pl.pallas_call(attend_kernel, out_shape=jax.ShapeDtypeStruct((SPAN, H * H...  59.7 us

profile of v3, /device:TPU:1, one launch (start us, length us, event | category | flops | bytes accessed | tf_op | source)
XLA Modules:
  0.0 60.6 jit_solution(4324714087224665898)
XLA Ops:
  0.0 59.7 %attend.1 = bf16[128,4096]{1,0:T(8,128)(2,1)S(1)} custom-call(s32[512]{0:T(512)} %anc_hbm.1, s32[512]{0:T(512)} %len_hbm.1, bf16[64,2,512]{2,1,0:T(2,128)(2,1)} %prompt_hbm.1, bf16[32,8,2,512]{3,2,1,0:T(2,128)(2,1)} %cache_hbm.1, bf16[128,4096]{1,0:T(8,128)(2,1)} %q_hbm.1, bf16[128,2,512]{2,1,0:T(2,128)(2,1)} %kvn_hbm.1), custom_call_target="tpu_custom_call" | custom-call | tf_op jit(solution)/shard_map/attend/pallas_call | solution.py:390
  59.7 1.0 %copy.8 = bf16[128,4096]{1,0:T(8,128)(2,1)} copy(bf16[128,4096]{1,0:T(8,128)(2,1)S(1)} %attend.1) | data formatting | bytes 2097152

commit v4 on v3

--- a/solution.py
+++ b/solution.py
@@ -270,14 +270,14 @@
 
         @pl.when(i == 11)
         def _():
+            ring_step(4, 0)
+            ring_step(4, 1)
             along_y(3)
 
         absorb_ring(q, pk, state, y, 1 + i // KVH, i % KVH)
         return carry
 
     lax.fori_loop(0, 3 * KVH, ring_part, 0)
-    ring_step(4, 0)
-    ring_step(4, 1)
     await_cores(4)
     limit = lens[anc[dom * PG + ctx]]
 

time: 60.8 us -> 60.2 us (level)
  no operation moved by 1% of the time
where the time goes in v4:
time: 60.2 us; the launch traced here: 60.1 us
  Pallas kernels  59.1 us (98%)
  local copies, waits for them, and re-layouts  0.97 us (2%)
    pallas_call x1, Pallas kernels, attend(): pl.pallas_call(attend_kernel, out_shape=jax.ShapeDtypeStruct((SPAN, H * H...  59.1 us

profile of v4, /device:TPU:1, one launch (start us, length us, event | category | flops | bytes accessed | tf_op | source)
XLA Modules:
  0.0 60.1 jit_solution(7629091219787947012)
XLA Ops:
  0.0 59.1 %attend.1 = bf16[128,4096]{1,0:T(8,128)(2,1)S(1)} custom-call(s32[512]{0:T(512)} %anc_hbm.1, s32[512]{0:T(512)} %len_hbm.1, bf16[64,2,512]{2,1,0:T(2,128)(2,1)} %prompt_hbm.1, bf16[32,8,2,512]{3,2,1,0:T(2,128)(2,1)} %cache_hbm.1, bf16[128,4096]{1,0:T(8,128)(2,1)} %q_hbm.1, bf16[128,2,512]{2,1,0:T(2,128)(2,1)} %kvn_hbm.1), custom_call_target="tpu_custom_call" | custom-call | tf_op jit(solution)/shard_map/attend/pallas_call | solution.py:390
  59.1 1.0 %copy.8 = bf16[128,4096]{1,0:T(8,128)(2,1)} copy(bf16[128,4096]{1,0:T(8,128)(2,1)S(1)} %attend.1) | data formatting | bytes 2097152
